TPU v7x, 32 devices: a whole 2x2x4 slice. The times are simulated.
32 devices in a mesh: layer: 2 (over z_hi), latent: 8 (over y, x, core), dp: 2 (over z_lo).
Axes of the slice: x: 2, y: 2, z: 4 (z_hi: 2, z_lo: 2; z = z_hi * 2 + z_lo), core: 2. Of those that a mesh axis runs over, the one named last changes fastest.
Arguments:
- layer_acts: bfloat16 [2, 128, 2560], P('layer', ('latent', 'dp')), may hold values from -6 to 6
- enc_weight: bfloat16 [2, 2560, 2048], P('layer', None, 'latent'), may hold values from -0.078125 to 0.078125
- dec_weight: bfloat16 [2, 2048, 2560], P('layer', 'latent'), may hold values from -0.125 to 0.125
- enc_bias: float32 [2048], P('latent'), may hold values from -3 to 3
- dec_bias: float32 [2, 2560], P('layer'), may hold values from -3 to 3
- block_ids: int32 [8, 16, 2], P('latent'), may hold values from 0 to 1, as said below
- block_counts: int32 [8, 16], P('latent'), may hold values from 1 to 2, as said below
Outputs:
- enc_grad: bfloat16 [2, 2560, 2048], P('layer', 'dp', 'latent')
- dec_grad: bfloat16 [2, 2048, 2560], P('layer', 'latent', 'dp')
- enc_bias_grad: float32 [2048], P(('latent', 'dp'))
- dec_bias_grad: float32 [2, 2560], P('layer', 'dp')
Inputs may be any that keep to these rules, and one draw needn't show every extreme that they name: block_ids[s, t] holds each of 0 .. 1 once. `block_counts`: every latent shard has a row tile with all 2 blocks active and one with a single active block.
All inputs are finite; a program needn't handle non-finite values.
Results may differ from a plain program's by a relative error of at most 0.02.
Values may be sent and summed in bfloat16 or wider, within the bound.
A program may use at most 64 MiB of HBM per device.

v0:
```python
import functools
import math

import jax
import jax.numpy as jnp
from jax import lax
from jax.experimental import pallas as pl
from jax.experimental.pallas import tpu as pltpu
from jax.sharding import PartitionSpec as P

SPARSITY = 0.5
NORM_EPS = 1e-06
MESH = pl.DeviceIdType.MESH
F32 = jnp.float32
BF16 = jnp.bfloat16
ENC_CHUNKS = 4
SPLITS = 1
CORES = 2


def step_kernel(
    n_layer, n_lat, n_dp,
    acts_hbm, enc_hbm, dec_hbm, ebias_hbm, dbias_hbm, ids_hbm, counts_hbm,
    acts_t, pg_out, dec_stage, eb_stage, db_stage,
    acts_all, enc_v, dec_v, ebias_v, dbias_v, ids_v, counts_v,
    acts_half, pre_send, pre_recv, codes_send, codes_recv,
    part_send, pair_recv, chip_send, part_recv, err_all, err_half, grad_send, grad_recv,
    pg_send, pg_recv,
    in_sems, acts_ss, acts_rs, ahalf_ss, ahalf_rs, pre_ss, pre_rs, codes_ss, codes_rs,
    pair_ss, pair_rs, part_ss, part_rs, err_ss, err_rs, ehalf_ss, ehalf_rs, grad_ss, grad_rs, pg_ss, pg_rs,
):
    layer = lax.axis_index("layer")
    me = lax.axis_index("latent")
    group = lax.axis_index("dp")
    rows = acts_all.shape[1]
    width = acts_all.shape[2]
    lat = enc_v.shape[1]
    blocks, tiles = ids_v.shape
    rows_group = rows * n_lat
    half = width // n_dp
    lat_part = lat // n_dp
    splits = acts_rs.shape[1]
    step = width // splits
    cuts = [slice(c * step, (c + 1) * step) for c in range(splits)]
    scale = 1.0 / math.sqrt(rows_group * n_dp)

    chips = n_lat // CORES
    chip = me // CORES
    core = lax.rem(me, CORES)
    partner = chip * CORES + 1 - core
    chip_peers = [lax.rem(chip + k, chips) for k in range(1, chips)]
    lat_peers = [lax.rem(me + k, n_lat) for k in range(1, n_lat)]
    layer_peers = [lax.rem(layer + k, n_layer) for k in range(1, n_layer)]
    dp_peers = [lax.rem(group + k, n_dp) for k in range(1, n_dp)]

    own_acts = pltpu.make_async_copy(acts_hbm.at[0], acts_all.at[me], in_sems.at[0])
    own_acts.start()
    loads = [
        pltpu.make_async_copy(src, dst, in_sems.at[i + 1])
        for i, (src, dst) in enumerate(
            (
                (enc_hbm.at[0], enc_v),
                (dec_hbm.at[0], dec_v),
                (ebias_hbm, ebias_v),
                (dbias_hbm, dbias_v),
                (ids_hbm.at[0], ids_v),
                (counts_hbm, counts_v),
            )
        )
    ]
    for load in loads:
        load.start()

    barrier = pltpu.get_barrier_semaphore()
    for p in lat_peers:
        pl.semaphore_signal(barrier, inc=1, device_id={"latent": p}, device_id_type=MESH)
    for p in layer_peers:
        pl.semaphore_signal(barrier, inc=1, device_id={"layer": p}, device_id_type=MESH)
    for p in dp_peers:
        pl.semaphore_signal(barrier, inc=1, device_id={"dp": p}, device_id_type=MESH)
    pl.semaphore_wait(barrier, n_lat + n_layer + n_dp - 3)

    def remote(src, dst, ss, rs, axis, peer):
        return pltpu.make_async_remote_copy(
            src_ref=src, dst_ref=dst, send_sem=ss, recv_sem=rs,
            device_id={axis: peer}, device_id_type=MESH,
        )

    sent = []

    def send(*args):
        copy = remote(*args)
        copy.start()
        sent.append(copy)

    def share(src, buf, ss, rs, c):
        dst = buf.at[me, :, cuts[c]]
        for k, q in enumerate(chip_peers):
            send(src, dst, ss.at[k, c], rs.at[me, c], "latent", q * CORES + core)
        send(src, dst, ss.at[chips - 1, c], rs.at[me, c], "latent", partner)

    def wait_cut(buf, ss, rs, j, c):
        part = buf.at[j, :, cuts[c]]
        remote(part, part, ss.at[0, c], rs.at[j, c], "latent", partner).wait_recv()

    def pass_on(buf, ss, rs, c):
        for k, q in enumerate(chip_peers):
            j = q * CORES + core
            wait_cut(buf, ss, rs, j, c)
            part = buf.at[j, :, cuts[c]]
            send(part, part, ss.at[chips + k, c], rs.at[j, c], "latent", partner)

    def gather_cuts(buf, ss, rs):
        pass_on(buf, ss, rs, 0)
        for c, cut in enumerate(cuts):
            if c + 1 < splits:
                pass_on(buf, ss, rs, c + 1)
            wait_cut(buf, ss, rs, partner, c)
            for q in chip_peers:
                wait_cut(buf, ss, rs, q * CORES + 1 - core, c)
            yield cut, buf[:, :, cut].astype(F32).reshape(rows_group, step).astype(BF16)

    for c, cut in enumerate(cuts):
        share(acts_hbm.at[0, :, cut], acts_all, acts_ss, acts_rs, c)

    for load in loads:
        load.wait()
    dec_f = dec_v[...].astype(F32)
    norm_col = jnp.sqrt(jnp.sum(dec_f * dec_f, axis=1, keepdims=True) + NORM_EPS)
    r_i = lax.broadcasted_iota(jnp.int32, (lat, lat), 0)
    c_i = lax.broadcasted_iota(jnp.int32, (lat, lat), 1)
    norm_row = jnp.sum(
        jnp.where(r_i == c_i, jnp.broadcast_to(norm_col, (lat, lat)), 0.0), axis=0, keepdims=True
    )
    ids_i = ids_v[...]
    counts_i = counts_v[...]
    lat_block = lax.broadcasted_iota(jnp.int32, (rows_group, lat), 1) // (lat // blocks)
    pick_r = lax.broadcasted_iota(jnp.int32, (rows_group, tiles), 0) // rows
    pick_c = lax.broadcasted_iota(jnp.int32, (rows_group, tiles), 1)
    picked = pick_c == pick_r * n_dp + group
    mask = jnp.zeros((rows_group, lat), F32)
    for b in range(blocks):
        hit = jnp.zeros((1, tiles), F32)
        for k in range(blocks):
            hit = jnp.where((ids_i[k : k + 1, :] == b) & (counts_i > k), 1.0, hit)
        row_hit = jnp.sum(
            jnp.where(picked, jnp.broadcast_to(hit, (rows_group, tiles)), 0.0), axis=1, keepdims=True
        )
        mask = jnp.where(lat_block == b, jnp.broadcast_to(row_hit, (rows_group, lat)), mask)

    own_acts.wait()

    def cross(src, dst_half, ss, rs):
        for q, p in enumerate(dp_peers):
            cols = pl.ds(pl.multiple_of(p * half, 128), half)
            send(src.at[:, cols], dst_half.at[group, me], ss.at[q, 0], rs.at[group, me], "dp", p)

    def wait_half(dst_half, ss, rs, p, j):
        remote(
            dst_half.at[p, j], dst_half.at[p, j], ss.at[0, 0], rs.at[p, j], "latent", lat_peers[0]
        ).wait_recv()

    def spread(dst_half, ss, rs):
        for q, p in enumerate(dp_peers):
            wait_half(dst_half, ss, rs, p, me)
            for k, j in enumerate(lat_peers):
                send(dst_half.at[p, me], dst_half.at[p, me], ss.at[q, k + 1], rs.at[p, me], "latent", j)

    cross(acts_all.at[me], acts_half, ahalf_ss, ahalf_rs)

    pre = jnp.zeros((rows_group, lat), F32)
    for cut, gathered in gather_cuts(acts_all, acts_ss, acts_rs):
        pre = pre + jnp.dot(gathered, enc_v[cut, :], preferred_element_type=F32)
    pre_send[...] = pre.astype(BF16)
    for k, p in enumerate(layer_peers):
        send(pre_send, pre_recv.at[layer], pre_ss.at[k], pre_rs.at[layer], "layer", p)
    spread(acts_half, ahalf_ss, ahalf_rs)
    pre = pre + ebias_v[...][None, :]
    for k, p in enumerate(layer_peers):
        remote(pre_send, pre_recv.at[p], pre_ss.at[k], pre_rs.at[p], "layer", p).wait_recv()
        pre = pre + pre_recv[p].astype(F32)

    codes = (jax.nn.softplus(pre) * mask).astype(BF16)
    codes_send[...] = codes
    def reduce_pair(c):
        cut = cuts[c]
        theirs = pair_recv.at[:, :, cut]
        remote(theirs, theirs, pair_ss.at[c], pair_rs.at[c], "latent", partner).wait_recv()
        total = part_send[core, :, :, cut].astype(F32) + pair_recv[:, :, cut].astype(F32)
        chip_send[:, :, cut] = total.astype(BF16)
        for k, q in enumerate(chip_peers):
            send(
                chip_send.at[q, :, cut], part_recv.at[chip, :, cut],
                part_ss.at[k, c], part_rs.at[chip, c], "latent", q * CORES + core,
            )

    for c, cut in enumerate(cuts):
        part = jnp.dot(codes, dec_v[:, cut], preferred_element_type=F32)
        part = part.reshape(chips, CORES, rows, step).astype(BF16)
        for d in range(CORES):
            part_send[d, :, :, cut] = part[:, d]
        send(
            part_send.at[1 - core, :, :, cut], pair_recv.at[:, :, cut],
            pair_ss.at[c], pair_rs.at[c], "latent", partner,
        )
        if c > 0:
            reduce_pair(c - 1)
    reduce_pair(splits - 1)
    for k, p in enumerate(dp_peers):
        send(codes_send, codes_recv.at[group], codes_ss.at[k], codes_rs.at[group], "dp", p)

    mine_cols = pl.ds(pl.multiple_of(group * half, 128), half)
    acts_rows = [acts_all[:, :, mine_cols].astype(F32).reshape(rows_group, half)]
    for q, p in enumerate(dp_peers):
        for j in lat_peers:
            wait_half(acts_half, ahalf_ss, ahalf_rs, p, j)
        acts_rows.append(acts_half[p].astype(F32).reshape(rows_group, half))
    acts_t[...] = jnp.concatenate(acts_rows, axis=0).T.astype(BF16)

    gate = mask * jax.nn.sigmoid(pre)

    for c, cut in enumerate(cuts):
        recon = part_send[core, chip, :, cut].astype(F32) + pair_recv[chip, :, cut].astype(F32)
        for q in chip_peers:
            wait_cut(part_recv, part_ss, part_rs, q, c)
            recon = recon + part_recv[q, :, cut].astype(F32)
        recon = recon + dbias_v[:, cut]
        err_all[me, :, cut] = (scale * (recon - acts_all[me, :, cut].astype(F32))).astype(BF16)
        share(err_all.at[me, :, cut], err_all, err_ss, err_rs, c)
    cross(err_all.at[me], err_half, ehalf_ss, ehalf_rs)

    code_rows = [codes.astype(F32)]
    for k, p in enumerate(dp_peers):
        remote(codes_send, codes_recv.at[p], codes_ss.at[k], codes_rs.at[p], "dp", p).wait_recv()
        code_rows.append(codes_recv[p].astype(F32))
    codes_t = jnp.concatenate(code_rows, axis=0).T
    totals = jnp.sum(codes_t, axis=1, keepdims=True)
    unit_gain = SPARSITY * scale * totals / norm_col
    codes_t = codes_t.astype(BF16)

    grad = jnp.zeros((rows_group, lat), F32)
    for cut, err in gather_cuts(err_all, err_ss, err_rs):
        grad = grad + lax.dot_general(
            err, dec_v[:, cut], (((1,), (1,)), ((), ())), preferred_element_type=F32
        )
    grad = grad + SPARSITY * scale * norm_row
    grad_send[...] = grad.astype(BF16)
    for k, p in enumerate(layer_peers):
        send(grad_send, grad_recv.at[layer], grad_ss.at[k], grad_rs.at[layer], "layer", p)
    spread(err_half, ehalf_ss, ehalf_rs)
    for k, p in enumerate(layer_peers):
        remote(grad_send, grad_recv.at[p], grad_ss.at[k], grad_rs.at[p], "layer", p).wait_recv()
        grad = grad + grad_recv[p].astype(F32)
    pre_grad = (grad * gate).astype(BF16)
    pg_send[...] = pre_grad
    for k, p in enumerate(dp_peers):
        send(pg_send, pg_recv.at[group], pg_ss.at[k], pg_rs.at[group], "dp", p)

    err_rows = [err_all[:, :, mine_cols].astype(F32).reshape(rows_group, half)]
    for q, p in enumerate(dp_peers):
        for j in lat_peers:
            wait_half(err_half, ehalf_ss, ehalf_rs, p, j)
        err_rows.append(err_half[p].astype(F32).reshape(rows_group, half))
    err_rows = jnp.concatenate(err_rows, axis=0)
    db_stage[...] = jnp.sum(err_rows, axis=0, keepdims=True)
    dec_grad = jnp.dot(codes_t, err_rows.astype(BF16), preferred_element_type=F32)
    dec_grad = dec_grad + unit_gain * dec_v[:, mine_cols].astype(F32)
    dec_stage[...] = dec_grad.astype(BF16)

    pg_rows = [pre_grad]
    for k, p in enumerate(dp_peers):
        remote(pg_send, pg_recv.at[p], pg_ss.at[k], pg_rs.at[p], "dp", p).wait_recv()
        pg_rows.append(pg_recv[p])
    pg_rows = jnp.concatenate(pg_rows, axis=0)
    pg_out[...] = pg_rows
    bias_sum = jnp.sum(pg_rows.astype(F32), axis=0, keepdims=True)
    bias_mine = bias_sum[:, :lat_part]
    for d in range(1, n_dp):
        bias_mine = jnp.where(group == d, bias_sum[:, d * lat_part : (d + 1) * lat_part], bias_mine)
    eb_stage[...] = bias_mine.reshape(lat_part)
    for copy in sent:
        copy.wait_send()


def finish_kernel(
    acts_t, pg_rows, dec_grad, eb_grad, db_grad, enc_out, dec_out, eb_out, db_out, enc_stage, sems
):
    copies = [
        pltpu.make_async_copy(dec_grad, dec_out.at[0], sems.at[0]),
        pltpu.make_async_copy(eb_grad, eb_out, sems.at[1]),
        pltpu.make_async_copy(db_grad, db_out, sems.at[2]),
    ]
    for copy in copies:
        copy.start()
    size = acts_t.shape[0] // ENC_CHUNKS
    for c in range(ENC_CHUNKS):
        part = pl.ds(c * size, size)
        enc_stage[part, :] = jnp.dot(
            acts_t[part, :], pg_rows[...], preferred_element_type=F32
        ).astype(BF16)
        copy = pltpu.make_async_copy(enc_stage.at[part, :], enc_out.at[0, part, :], sems.at[3 + c])
        copy.start()
        copies.append(copy)
    for copy in copies:
        copy.wait()


def on_device(layer_acts, enc_weight, dec_weight, enc_bias, dec_bias, block_ids, block_counts):
    n_layer = lax.axis_size("layer")
    n_lat = lax.axis_size("latent")
    n_dp = lax.axis_size("dp")
    rows, width = layer_acts.shape[1:]
    lat = enc_weight.shape[2]
    tiles, blocks = block_ids.shape[1:]
    group_rows = rows * n_lat
    chips = n_lat // CORES
    splits = SPLITS if width % (128 * SPLITS) == 0 else 1
    half = width // n_dp
    any_spec = pl.BlockSpec(memory_space=pltpu.HBM)
    vmem_spec = pl.BlockSpec(memory_space=pltpu.VMEM)
    dma = lambda *shape: pltpu.SemaphoreType.DMA(shape)
    staged = pl.pallas_call(
        functools.partial(step_kernel, n_layer, n_lat, n_dp),
        out_shape=(
            pltpu.VMEM((half, n_dp * group_rows), BF16),
            pltpu.VMEM((n_dp * group_rows, lat), BF16),
            pltpu.VMEM((lat, half), BF16),
            pltpu.VMEM((lat // n_dp,), F32),
            pltpu.VMEM((1, half), F32),
        ),
        in_specs=[any_spec] * 7,
        out_specs=(vmem_spec,) * 5,
        scratch_shapes=[
            pltpu.VMEM((n_lat, rows, width), BF16),
            pltpu.VMEM((width, lat), BF16),
            pltpu.VMEM((lat, width), BF16),
            pltpu.VMEM((lat,), F32),
            pltpu.VMEM((1, width), F32),
            pltpu.VMEM((blocks, tiles), jnp.int32),
            pltpu.VMEM((1, tiles), jnp.int32),
            pltpu.VMEM((n_dp, n_lat, rows, half), BF16),
            pltpu.VMEM((group_rows, lat), BF16),
            pltpu.VMEM((n_layer, group_rows, lat), BF16),
            pltpu.VMEM((group_rows, lat), BF16),
            pltpu.VMEM((n_dp, group_rows, lat), BF16),
            pltpu.VMEM((CORES, chips, rows, width), BF16),
            pltpu.VMEM((chips, rows, width), BF16),
            pltpu.VMEM((chips, rows, width), BF16),
            pltpu.VMEM((chips, rows, width), BF16),
            pltpu.VMEM((n_lat, rows, width), BF16),
            pltpu.VMEM((n_dp, n_lat, rows, half), BF16),
            pltpu.VMEM((group_rows, lat), BF16),
            pltpu.VMEM((n_layer, group_rows, lat), BF16),
            pltpu.VMEM((group_rows, lat), BF16),
            pltpu.VMEM((n_dp, group_rows, lat), BF16),
            dma(7),
            dma(2 * chips - 1, splits), dma(n_lat, splits),
            dma(n_dp - 1, n_lat), dma(n_dp, n_lat),
            dma(n_layer - 1), dma(n_layer),
            dma(n_dp - 1), dma(n_dp),
            dma(splits), dma(splits),
            dma(chips - 1, splits), dma(chips, splits),
            dma(2 * chips - 1, splits), dma(n_lat, splits),
            dma(n_dp - 1, n_lat), dma(n_dp, n_lat),
            dma(n_layer - 1), dma(n_layer),
            dma(n_dp - 1), dma(n_dp),
        ],
        compiler_params=pltpu.CompilerParams(
            collective_id=0, has_side_effects=True, vmem_limit_bytes=40 << 20
        ),
        name="crosscoder_step",
    )(*[
        pltpu.with_memory_space_constraint(x, pltpu.HBM)
        for x in (
            layer_acts, enc_weight, dec_weight, enc_bias, dec_bias,
            jnp.swapaxes(block_ids, 1, 2), block_counts,
        )
    ])
    return pl.pallas_call(
        finish_kernel,
        out_shape=(
            jax.ShapeDtypeStruct((1, half, lat), BF16),
            jax.ShapeDtypeStruct((1, lat, half), BF16),
            jax.ShapeDtypeStruct((lat // n_dp,), F32),
            jax.ShapeDtypeStruct((1, half), F32),
        ),
        in_specs=[vmem_spec] * 5,
        out_specs=(any_spec,) * 4,
        scratch_shapes=[pltpu.VMEM((half, lat), BF16), dma(3 + ENC_CHUNKS)],
        compiler_params=pltpu.CompilerParams(vmem_limit_bytes=16 << 20),
        name="crosscoder_finish",
    )(*staged)


def solution(mesh):
    in_specs = (
        P("layer", ("latent", "dp"), None),
        P("layer", None, "latent"),
        P("layer", "latent", None),
        P("latent"),
        P("layer", None),
        P("latent", None, None),
        P("latent", None),
    )
    out_specs = (
        P("layer", "dp", "latent"),
        P("layer", "latent", "dp"),
        P(("latent", "dp")),
        P("layer", "dp"),
    )
    return jax.shard_map(
        on_device, mesh=mesh, in_specs=in_specs, out_specs=out_specs, check_vma=False
    )
```

profile of v0, /device:TPU:0, one launch (start us, length us, event | category | flops | bytes accessed | tf_op | source)
XLA Modules:
  0.0 33.5 jit_solution(17312873674455319297)
XLA Ops:
  0.6 31.7 %crosscoder_step.1 = (bf16[1280,128]{1,0:T(8,128)(2,1)S(1)}, bf16[128,256]{1,0:T(8,128)(2,1)S(1)}, bf16[256,1280]{1,0:T(8,128)(2,1)S(1)}, f32[128]{0:T(128)S(1)}, f32[1,1280]{1,0:T(1,128)S(1)}) custom-call(bf16[1,8,2560]{2,1,0:T(8,128)(2,1)} %acts_hbm.1, bf16[1,2560,256]{2,1,0:T(8,128)(2,1)} %enc_hbm.1, bf16[1,256,2560]{2,1,0:T(8,128)(2,1)} %dec_hbm.1, ...), custom_call_target="tpu_custom_call" | custom-call | tf_op jit(solution)/shard_map/crosscoder_step/pallas_call | solution.py:322
  32.3 1.1 %crosscoder_finish.1 = (bf16[1,1280,256]{2,1,0:T(8,128)(2,1)}, bf16[1,256,1280]{2,1,0:T(8,128)(2,1)}, f32[128]{0:T(128)}, f32[1,1280]{1,0:T(1,128)}) custom-call(bf16[1280,128]{1,0:T(8,128)(2,1)S(1)} %get-tuple-element.9.acts_t, bf16[128,256]{1,0:T(8,128)(2,1)S(1)} %get-tuple-element.10.pg_rows, bf16[256,1280]{1,0:T(8,128)(2,1)S(1)} %get-tuple-element.11.dec_grad, ...), custom_call_target="tpu_custom_call" | custom-call | tf_op jit(solution)/shard_map/crosscoder_finish/pallas_call | solution.py:379
where the time goes:
time: 33.6 us; the launch traced here: 33.5 us
  Pallas kernels  32.8 us (98%)
  between operations  0.64 us (2%)
    pallas_call x1, Pallas kernels, on_device(): pl.pallas_call(functools.partial(step_kernel, n_layer, n_lat, n_dp), out_...  31.7 us
    pallas_call x1, Pallas kernels, on_device(): pl.pallas_call(finish_kernel, out_shape=(jax.ShapeDtypeStruct((1, half, l...  1.12 us

commit v1 on v0

--- a/solution.py
+++ b/solution.py
@@ -18,6 +18,19 @@
 CORES = 2
 
 
+def far_first(index, size):
+    if size & (size - 1):
+        return [lax.rem(index + k, size) for k in range(1, size)]
+    peers = []
+    for k in sorted(range(1, size), key=lambda k: (-bin(k).count("1"), -k)):
+        peer = index
+        for b in range(size.bit_length() - 1):
+            if k >> b & 1:
+                peer = peer + (1 << b) - (2 << b) * lax.rem(index // (1 << b), 2)
+        peers.append(peer)
+    return peers
+
+
 def step_kernel(
     n_layer, n_lat, n_dp,
     acts_hbm, enc_hbm, dec_hbm, ebias_hbm, dbias_hbm, ids_hbm, counts_hbm,
@@ -25,9 +38,9 @@
     acts_all, enc_v, dec_v, ebias_v, dbias_v, ids_v, counts_v,
     acts_half, pre_send, pre_recv, codes_send, codes_recv,
     part_send, pair_recv, chip_send, part_recv, err_all, err_half, grad_send, grad_recv,
-    pg_send, pg_recv,
+    gate_send, gate_recv,
     in_sems, acts_ss, acts_rs, ahalf_ss, ahalf_rs, pre_ss, pre_rs, codes_ss, codes_rs,
-    pair_ss, pair_rs, part_ss, part_rs, err_ss, err_rs, ehalf_ss, ehalf_rs, grad_ss, grad_rs, pg_ss, pg_rs,
+    pair_ss, pair_rs, part_ss, part_rs, err_ss, err_rs, ehalf_ss, ehalf_rs, grad_ss, grad_rs, gate_ss, gate_rs,
 ):
     layer = lax.axis_index("layer")
     me = lax.axis_index("latent")
@@ -48,10 +61,12 @@
     chip = me // CORES
     core = lax.rem(me, CORES)
     partner = chip * CORES + 1 - core
-    chip_peers = [lax.rem(chip + k, chips) for k in range(1, chips)]
+    chip_peers = far_first(chip, chips)
     lat_peers = [lax.rem(me + k, n_lat) for k in range(1, n_lat)]
     layer_peers = [lax.rem(layer + k, n_layer) for k in range(1, n_layer)]
     dp_peers = [lax.rem(group + k, n_dp) for k in range(1, n_dp)]
+    z_peers = [(p, d) for p in layer_peers for d in dp_peers]
+    z_peers += [(p, group) for p in layer_peers] + [(layer, d) for d in dp_peers]
 
     own_acts = pltpu.make_async_copy(acts_hbm.at[0], acts_all.at[me], in_sems.at[0])
     own_acts.start()
@@ -74,11 +89,9 @@
     barrier = pltpu.get_barrier_semaphore()
     for p in lat_peers:
         pl.semaphore_signal(barrier, inc=1, device_id={"latent": p}, device_id_type=MESH)
-    for p in layer_peers:
-        pl.semaphore_signal(barrier, inc=1, device_id={"layer": p}, device_id_type=MESH)
-    for p in dp_peers:
-        pl.semaphore_signal(barrier, inc=1, device_id={"dp": p}, device_id_type=MESH)
-    pl.semaphore_wait(barrier, n_lat + n_layer + n_dp - 3)
+    for p, d in z_peers:
+        pl.semaphore_signal(barrier, inc=1, device_id={"layer": p, "dp": d}, device_id_type=MESH)
+    pl.semaphore_wait(barrier, len(lat_peers) + len(z_peers))
 
     def remote(src, dst, ss, rs, axis, peer):
         return pltpu.make_async_remote_copy(
@@ -110,18 +123,25 @@
             part = buf.at[j, :, cuts[c]]
             send(part, part, ss.at[chips + k, c], rs.at[j, c], "latent", partner)
 
-    def gather_cuts(buf, ss, rs):
-        pass_on(buf, ss, rs, 0)
+    def gather_cuts(buf, ss, rs, beside):
+        for c in range(splits):
+            pass_on(buf, ss, rs, c)
+        beside()
         for c, cut in enumerate(cuts):
-            if c + 1 < splits:
-                pass_on(buf, ss, rs, c + 1)
             wait_cut(buf, ss, rs, partner, c)
             for q in chip_peers:
                 wait_cut(buf, ss, rs, q * CORES + 1 - core, c)
             yield cut, buf[:, :, cut].astype(F32).reshape(rows_group, step).astype(BF16)
 
+    def cross(src, dst_half, ss, rs):
+        for q, p in enumerate(dp_peers):
+            cols = pl.ds(pl.multiple_of(p * half, 128), half)
+            send(src.at[:, cols], dst_half.at[group, me], ss.at[q, 0], rs.at[group, me], "dp", p)
+
+    own_acts.wait()
     for c, cut in enumerate(cuts):
-        share(acts_hbm.at[0, :, cut], acts_all, acts_ss, acts_rs, c)
+        share(acts_all.at[me, :, cut], acts_all, acts_ss, acts_rs, c)
+    cross(acts_all.at[me], acts_half, ahalf_ss, ahalf_rs)
 
     for load in loads:
         load.wait()
@@ -148,13 +168,6 @@
         )
         mask = jnp.where(lat_block == b, jnp.broadcast_to(row_hit, (rows_group, lat)), mask)
 
-    own_acts.wait()
-
-    def cross(src, dst_half, ss, rs):
-        for q, p in enumerate(dp_peers):
-            cols = pl.ds(pl.multiple_of(p * half, 128), half)
-            send(src.at[:, cols], dst_half.at[group, me], ss.at[q, 0], rs.at[group, me], "dp", p)
-
     def wait_half(dst_half, ss, rs, p, j):
         remote(
             dst_half.at[p, j], dst_half.at[p, j], ss.at[0, 0], rs.at[p, j], "latent", lat_peers[0]
@@ -166,10 +179,8 @@
             for k, j in enumerate(lat_peers):
                 send(dst_half.at[p, me], dst_half.at[p, me], ss.at[q, k + 1], rs.at[p, me], "latent", j)
 
-    cross(acts_all.at[me], acts_half, ahalf_ss, ahalf_rs)
-
     pre = jnp.zeros((rows_group, lat), F32)
-    for cut, gathered in gather_cuts(acts_all, acts_ss, acts_rs):
+    for cut, gathered in gather_cuts(acts_all, acts_ss, acts_rs, lambda: None):
         pre = pre + jnp.dot(gathered, enc_v[cut, :], preferred_element_type=F32)
     pre_send[...] = pre.astype(BF16)
     for k, p in enumerate(layer_peers):
@@ -218,6 +229,9 @@
     acts_t[...] = jnp.concatenate(acts_rows, axis=0).T.astype(BF16)
 
     gate = mask * jax.nn.sigmoid(pre)
+    gate_send[...] = gate.astype(BF16)
+    for k, p in enumerate(dp_peers):
+        send(gate_send, gate_recv.at[group], gate_ss.at[k], gate_rs.at[group], "dp", p)
 
     for c, cut in enumerate(cuts):
         recon = part_send[core, chip, :, cut].astype(F32) + pair_recv[chip, :, cut].astype(F32)
@@ -239,22 +253,20 @@
     codes_t = codes_t.astype(BF16)
 
     grad = jnp.zeros((rows_group, lat), F32)
-    for cut, err in gather_cuts(err_all, err_ss, err_rs):
+    for cut, err in gather_cuts(err_all, err_ss, err_rs, lambda: spread(err_half, ehalf_ss, ehalf_rs)):
         grad = grad + lax.dot_general(
             err, dec_v[:, cut], (((1,), (1,)), ((), ())), preferred_element_type=F32
         )
     grad = grad + SPARSITY * scale * norm_row
     grad_send[...] = grad.astype(BF16)
-    for k, p in enumerate(layer_peers):
-        send(grad_send, grad_recv.at[layer], grad_ss.at[k], grad_rs.at[layer], "layer", p)
-    spread(err_half, ehalf_ss, ehalf_rs)
-    for k, p in enumerate(layer_peers):
-        remote(grad_send, grad_recv.at[p], grad_ss.at[k], grad_rs.at[p], "layer", p).wait_recv()
-        grad = grad + grad_recv[p].astype(F32)
-    pre_grad = (grad * gate).astype(BF16)
-    pg_send[...] = pre_grad
-    for k, p in enumerate(dp_peers):
-        send(pg_send, pg_recv.at[group], pg_ss.at[k], pg_rs.at[group], "dp", p)
+    for k, (p, d) in enumerate(z_peers):
+        copy = pltpu.make_async_remote_copy(
+            src_ref=grad_send, dst_ref=grad_recv.at[layer, group],
+            send_sem=grad_ss.at[k], recv_sem=grad_rs.at[layer, group],
+            device_id={"layer": p, "dp": d}, device_id_type=MESH,
+        )
+        copy.start()
+        sent.append(copy)
 
     err_rows = [err_all[:, :, mine_cols].astype(F32).reshape(rows_group, half)]
     for q, p in enumerate(dp_peers):
@@ -267,10 +279,23 @@
     dec_grad = dec_grad + unit_gain * dec_v[:, mine_cols].astype(F32)
     dec_stage[...] = dec_grad.astype(BF16)
 
-    pg_rows = [pre_grad]
-    for k, p in enumerate(dp_peers):
-        remote(pg_send, pg_recv.at[p], pg_ss.at[k], pg_rs.at[p], "dp", p).wait_recv()
-        pg_rows.append(pg_recv[p])
+    gates = [gate]
+    for k, d in enumerate(dp_peers):
+        remote(gate_send, gate_recv.at[d], gate_ss.at[k], gate_rs.at[d], "dp", d).wait_recv()
+        gates.append(gate_recv[d].astype(F32))
+
+    def wait_grad(p, d):
+        remote(grad_send, grad_recv.at[p, d], grad_ss.at[0], grad_rs.at[p, d], "latent", partner).wait_recv()
+        return grad_recv[p, d].astype(F32)
+
+    for p in layer_peers:
+        grad = grad + wait_grad(p, group)
+    pg_rows = [(grad * gates[0]).astype(BF16)]
+    for k, d in enumerate(dp_peers):
+        other = wait_grad(layer, d)
+        for p in layer_peers:
+            other = other + wait_grad(p, d)
+        pg_rows.append((other * gates[k + 1]).astype(BF16))
     pg_rows = jnp.concatenate(pg_rows, axis=0)
     pg_out[...] = pg_rows
     bias_sum = jnp.sum(pg_rows.astype(F32), axis=0, keepdims=True)
@@ -350,7 +375,7 @@
             pltpu.VMEM((n_lat, rows, width), BF16),
             pltpu.VMEM((n_dp, n_lat, rows, half), BF16),
             pltpu.VMEM((group_rows, lat), BF16),
-            pltpu.VMEM((n_layer, group_rows, lat), BF16),
+            pltpu.VMEM((n_layer, n_dp, group_rows, lat), BF16),
             pltpu.VMEM((group_rows, lat), BF16),
             pltpu.VMEM((n_dp, group_rows, lat), BF16),
             dma(7),
@@ -362,7 +387,7 @@
             dma(chips - 1, splits), dma(chips, splits),
             dma(2 * chips - 1, splits), dma(n_lat, splits),
             dma(n_dp - 1, n_lat), dma(n_dp, n_lat),
-            dma(n_layer - 1), dma(n_layer),
+            dma(n_layer * n_dp - 1), dma(n_layer, n_dp),
             dma(n_dp - 1), dma(n_dp),
         ],
         compiler_params=pltpu.CompilerParams(

time: 33.6 us -> 32 us (0.952)
  Pallas kernels: 32.8 us -> 31.2 us
    pallas_call x1, Pallas kernels: 31.7 us -> 30.1 us  [on_device(): pl.pallas_call(functools.partial(step_kernel, n_layer, n_lat, n_dp), out_...]
where the time goes in v1:
time: 32 us; the launch traced here: 31.9 us
  Pallas kernels  31.2 us (98%)
  between operations  0.64 us (2%)
    pallas_call x1, Pallas kernels, on_device(): pl.pallas_call(functools.partial(step_kernel, n_layer, n_lat, n_dp), out_...  30.1 us
    pallas_call x1, Pallas kernels, on_device(): pl.pallas_call(finish_kernel, out_shape=(jax.ShapeDtypeStruct((1, half, l...  1.12 us

profile of v1, /device:TPU:0, one launch (start us, length us, event | category | flops | bytes accessed | tf_op | source)
XLA Modules:
  0.0 31.9 jit_solution(18116797806988853870)
XLA Ops:
  0.6 30.1 %crosscoder_step.1 = (bf16[1280,128]{1,0:T(8,128)(2,1)S(1)}, bf16[128,256]{1,0:T(8,128)(2,1)S(1)}, bf16[256,1280]{1,0:T(8,128)(2,1)S(1)}, f32[128]{0:T(128)S(1)}, f32[1,1280]{1,0:T(1,128)S(1)}) custom-call(bf16[1,8,2560]{2,1,0:T(8,128)(2,1)} %acts_hbm.1, bf16[1,2560,256]{2,1,0:T(8,128)(2,1)} %enc_hbm.1, bf16[1,256,2560]{2,1,0:T(8,128)(2,1)} %dec_hbm.1, ...), custom_call_target="tpu_custom_call" | custom-call | tf_op jit(solution)/shard_map/crosscoder_step/pallas_call | solution.py:347
  30.8 1.1 %crosscoder_finish.1 = (bf16[1,1280,256]{2,1,0:T(8,128)(2,1)}, bf16[1,256,1280]{2,1,0:T(8,128)(2,1)}, f32[128]{0:T(128)}, f32[1,1280]{1,0:T(1,128)}) custom-call(bf16[1280,128]{1,0:T(8,128)(2,1)S(1)} %get-tuple-element.9.acts_t, bf16[128,256]{1,0:T(8,128)(2,1)S(1)} %get-tuple-element.10.pg_rows, bf16[256,1280]{1,0:T(8,128)(2,1)S(1)} %get-tuple-element.11.dec_grad, ...), custom_call_target="tpu_custom_call" | custom-call | tf_op jit(solution)/shard_map/crosscoder_finish/pallas_call | solution.py:404

commit v2 on v1

--- a/solution.py
+++ b/solution.py
@@ -14,19 +14,18 @@
 F32 = jnp.float32
 BF16 = jnp.bfloat16
 ENC_CHUNKS = 4
-SPLITS = 1
 CORES = 2
 
 
-def far_first(index, size):
-    if size & (size - 1):
-        return [lax.rem(index + k, size) for k in range(1, size)]
+def chip_peers_of(chip, chips):
+    if chips & (chips - 1):
+        return [lax.rem(chip + k, chips) for k in range(1, chips)]
     peers = []
-    for k in sorted(range(1, size), key=lambda k: (-bin(k).count("1"), -k)):
-        peer = index
-        for b in range(size.bit_length() - 1):
+    for k in sorted(range(1, chips), key=lambda k: (-bin(k).count("1"), -k)):
+        peer = chip
+        for b in range(chips.bit_length() - 1):
             if k >> b & 1:
-                peer = peer + (1 << b) - (2 << b) * lax.rem(index // (1 << b), 2)
+                peer = peer + (1 << b) - (2 << b) * lax.rem(chip // (1 << b), 2)
         peers.append(peer)
     return peers
 
@@ -36,7 +35,7 @@
     acts_hbm, enc_hbm, dec_hbm, ebias_hbm, dbias_hbm, ids_hbm, counts_hbm,
     acts_t, pg_out, dec_stage, eb_stage, db_stage,
     acts_all, enc_v, dec_v, ebias_v, dbias_v, ids_v, counts_v,
-    acts_half, pre_send, pre_recv, codes_send, codes_recv,
+    dec_t, acts_half, pre_send, pre_recv, codes_send, codes_recv,
     part_send, pair_recv, chip_send, part_recv, err_all, err_half, grad_send, grad_recv,
     gate_send, gate_recv,
     in_sems, acts_ss, acts_rs, ahalf_ss, ahalf_rs, pre_ss, pre_rs, codes_ss, codes_rs,
@@ -52,21 +51,21 @@
     rows_group = rows * n_lat
     half = width // n_dp
     lat_part = lat // n_dp
-    splits = acts_rs.shape[1]
-    step = width // splits
-    cuts = [slice(c * step, (c + 1) * step) for c in range(splits)]
     scale = 1.0 / math.sqrt(rows_group * n_dp)
 
     chips = n_lat // CORES
     chip = me // CORES
     core = lax.rem(me, CORES)
     partner = chip * CORES + 1 - core
-    chip_peers = far_first(chip, chips)
+    chip_peers = chip_peers_of(chip, chips)
+    n_peers = len(chip_peers)
     lat_peers = [lax.rem(me + k, n_lat) for k in range(1, n_lat)]
     layer_peers = [lax.rem(layer + k, n_layer) for k in range(1, n_layer)]
     dp_peers = [lax.rem(group + k, n_dp) for k in range(1, n_dp)]
-    z_peers = [(p, d) for p in layer_peers for d in dp_peers]
-    z_peers += [(p, group) for p in layer_peers] + [(layer, d) for d in dp_peers]
+    n_z = n_layer * n_dp
+    rank = layer * n_dp + group
+    others = [i + lax.div(i - rank + n_z, n_z) for i in range(n_z - 1)]
+    z_peers = [(lax.div(i, n_dp), lax.rem(i, n_dp)) for i in others]
 
     own_acts = pltpu.make_async_copy(acts_hbm.at[0], acts_all.at[me], in_sems.at[0])
     own_acts.start()
@@ -91,7 +90,8 @@
         pl.semaphore_signal(barrier, inc=1, device_id={"latent": p}, device_id_type=MESH)
     for p, d in z_peers:
         pl.semaphore_signal(barrier, inc=1, device_id={"layer": p, "dp": d}, device_id_type=MESH)
-    pl.semaphore_wait(barrier, len(lat_peers) + len(z_peers))
+    with jax.named_scope("entry"):
+        pl.semaphore_wait(barrier, len(lat_peers) + len(z_peers))
 
     def remote(src, dst, ss, rs, axis, peer):
         return pltpu.make_async_remote_copy(
@@ -106,32 +106,29 @@
         copy.start()
         sent.append(copy)
 
-    def share(src, buf, ss, rs, c):
-        dst = buf.at[me, :, cuts[c]]
+    def share(buf, ss, rs):
+        mine = buf.at[me]
+        targets = [q * CORES + 1 - core for q in chip_peers] + [partner]
+        for k, j in enumerate(targets):
+            send(mine, mine, ss.at[k], rs.at[me], "latent", j)
+
+    def wait_block(buf, ss, rs, j):
+        remote(buf.at[j], buf.at[j], ss.at[0], rs.at[j], "latent", partner).wait_recv()
+
+    def gather(buf, ss, rs, beside):
         for k, q in enumerate(chip_peers):
-            send(src, dst, ss.at[k, c], rs.at[me, c], "latent", q * CORES + core)
-        send(src, dst, ss.at[chips - 1, c], rs.at[me, c], "latent", partner)
-
-    def wait_cut(buf, ss, rs, j, c):
-        part = buf.at[j, :, cuts[c]]
-        remote(part, part, ss.at[0, c], rs.at[j, c], "latent", partner).wait_recv()
-
-    def pass_on(buf, ss, rs, c):
-        for k, q in enumerate(chip_peers):
-            j = q * CORES + core
-            wait_cut(buf, ss, rs, j, c)
-            part = buf.at[j, :, cuts[c]]
-            send(part, part, ss.at[chips + k, c], rs.at[j, c], "latent", partner)
-
-    def gather_cuts(buf, ss, rs, beside):
-        for c in range(splits):
-            pass_on(buf, ss, rs, c)
+            j = q * CORES + 1 - core
+            with jax.named_scope("relay"):
+                wait_block(buf, ss, rs, j)
+            send(buf.at[j], buf.at[j], ss.at[n_peers + 1 + k], rs.at[j], "latent", partner)
         beside()
-        for c, cut in enumerate(cuts):
-            wait_cut(buf, ss, rs, partner, c)
+        with jax.named_scope("direct"):
+            for j in [partner]:
+                wait_block(buf, ss, rs, j)
+        with jax.named_scope("relayed"):
             for q in chip_peers:
-                wait_cut(buf, ss, rs, q * CORES + 1 - core, c)
-            yield cut, buf[:, :, cut].astype(F32).reshape(rows_group, step).astype(BF16)
+                wait_block(buf, ss, rs, q * CORES + core)
+        return buf[...].astype(F32).reshape(rows_group, width).astype(BF16)
 
     def cross(src, dst_half, ss, rs):
         for q, p in enumerate(dp_peers):
@@ -139,8 +136,7 @@
             send(src.at[:, cols], dst_half.at[group, me], ss.at[q, 0], rs.at[group, me], "dp", p)
 
     own_acts.wait()
-    for c, cut in enumerate(cuts):
-        share(acts_all.at[me, :, cut], acts_all, acts_ss, acts_rs, c)
+    share(acts_all, acts_ss, acts_rs)
     cross(acts_all.at[me], acts_half, ahalf_ss, ahalf_rs)
 
     for load in loads:
@@ -152,6 +148,7 @@
     norm_row = jnp.sum(
         jnp.where(r_i == c_i, jnp.broadcast_to(norm_col, (lat, lat)), 0.0), axis=0, keepdims=True
     )
+    dec_t[...] = dec_v[...].T
     ids_i = ids_v[...]
     counts_i = counts_v[...]
     lat_block = lax.broadcasted_iota(jnp.int32, (rows_group, lat), 1) // (lat // blocks)
@@ -175,55 +172,53 @@
 
     def spread(dst_half, ss, rs):
         for q, p in enumerate(dp_peers):
-            wait_half(dst_half, ss, rs, p, me)
+            with jax.named_scope("half"):
+                wait_half(dst_half, ss, rs, p, me)
             for k, j in enumerate(lat_peers):
                 send(dst_half.at[p, me], dst_half.at[p, me], ss.at[q, k + 1], rs.at[p, me], "latent", j)
 
-    pre = jnp.zeros((rows_group, lat), F32)
-    for cut, gathered in gather_cuts(acts_all, acts_ss, acts_rs, lambda: None):
-        pre = pre + jnp.dot(gathered, enc_v[cut, :], preferred_element_type=F32)
+    gathered = gather(acts_all, acts_ss, acts_rs, lambda: None)
+    pre = jnp.dot(gathered, enc_v[...], preferred_element_type=F32)
     pre_send[...] = pre.astype(BF16)
     for k, p in enumerate(layer_peers):
         send(pre_send, pre_recv.at[layer], pre_ss.at[k], pre_rs.at[layer], "layer", p)
     spread(acts_half, ahalf_ss, ahalf_rs)
     pre = pre + ebias_v[...][None, :]
     for k, p in enumerate(layer_peers):
-        remote(pre_send, pre_recv.at[p], pre_ss.at[k], pre_rs.at[p], "layer", p).wait_recv()
+        with jax.named_scope("layers"):
+            remote(pre_send, pre_recv.at[p], pre_ss.at[k], pre_rs.at[p], "layer", p).wait_recv()
         pre = pre + pre_recv[p].astype(F32)
 
     codes = (jax.nn.softplus(pre) * mask).astype(BF16)
     codes_send[...] = codes
-    def reduce_pair(c):
-        cut = cuts[c]
-        theirs = pair_recv.at[:, :, cut]
-        remote(theirs, theirs, pair_ss.at[c], pair_rs.at[c], "latent", partner).wait_recv()
-        total = part_send[core, :, :, cut].astype(F32) + pair_recv[:, :, cut].astype(F32)
-        chip_send[:, :, cut] = total.astype(BF16)
-        for k, q in enumerate(chip_peers):
-            send(
-                chip_send.at[q, :, cut], part_recv.at[chip, :, cut],
-                part_ss.at[k, c], part_rs.at[chip, c], "latent", q * CORES + core,
-            )
-
-    for c, cut in enumerate(cuts):
-        part = jnp.dot(codes, dec_v[:, cut], preferred_element_type=F32)
-        part = part.reshape(chips, CORES, rows, step).astype(BF16)
-        for d in range(CORES):
-            part_send[d, :, :, cut] = part[:, d]
+    part = jnp.dot(codes, dec_v[...], preferred_element_type=F32)
+    part_send[...] = part.reshape(n_lat, rows, width).astype(BF16)
+    for k, q in enumerate(chip_peers):
         send(
-            part_send.at[1 - core, :, :, cut], pair_recv.at[:, :, cut],
-            pair_ss.at[c], pair_rs.at[c], "latent", partner,
-        )
-        if c > 0:
-            reduce_pair(c - 1)
-    reduce_pair(splits - 1)
+            part_send.at[q * CORES + core], pair_recv.at[k],
+            pair_ss.at[k], pair_rs.at[k], "latent", partner,
+        )
+    for k, j in enumerate([partner]):
+        send(part_send.at[j], part_recv.at[me], part_ss.at[n_peers + k], part_rs.at[me], "latent", j)
+    for k, q in enumerate(chip_peers):
+        with jax.named_scope("pair"):
+            remote(
+                pair_recv.at[k], pair_recv.at[k], pair_ss.at[k], pair_rs.at[k], "latent", partner
+            ).wait_recv()
+        total = part_send[q * CORES + 1 - core].astype(F32) + pair_recv[k].astype(F32)
+        chip_send[k] = total.astype(BF16)
+        send(
+            chip_send.at[k], part_recv.at[me], part_ss.at[k], part_rs.at[me],
+            "latent", q * CORES + 1 - core,
+        )
     for k, p in enumerate(dp_peers):
         send(codes_send, codes_recv.at[group], codes_ss.at[k], codes_rs.at[group], "dp", p)
 
     mine_cols = pl.ds(pl.multiple_of(group * half, 128), half)
     acts_rows = [acts_all[:, :, mine_cols].astype(F32).reshape(rows_group, half)]
     for q, p in enumerate(dp_peers):
-        for j in lat_peers:
+        with jax.named_scope("halves"):
+          for j in lat_peers:
             wait_half(acts_half, ahalf_ss, ahalf_rs, p, j)
         acts_rows.append(acts_half[p].astype(F32).reshape(rows_group, half))
     acts_t[...] = jnp.concatenate(acts_rows, axis=0).T.astype(BF16)
@@ -233,14 +228,13 @@
     for k, p in enumerate(dp_peers):
         send(gate_send, gate_recv.at[group], gate_ss.at[k], gate_rs.at[group], "dp", p)
 
-    for c, cut in enumerate(cuts):
-        recon = part_send[core, chip, :, cut].astype(F32) + pair_recv[chip, :, cut].astype(F32)
-        for q in chip_peers:
-            wait_cut(part_recv, part_ss, part_rs, q, c)
-            recon = recon + part_recv[q, :, cut].astype(F32)
-        recon = recon + dbias_v[:, cut]
-        err_all[me, :, cut] = (scale * (recon - acts_all[me, :, cut].astype(F32))).astype(BF16)
-        share(err_all.at[me, :, cut], err_all, err_ss, err_rs, c)
+    recon = part_send[me].astype(F32) + dbias_v[...]
+    for j in [partner] + [q * CORES + 1 - core for q in chip_peers]:
+        with jax.named_scope("chips"):
+            wait_block(part_recv, part_ss, part_rs, j)
+        recon = recon + part_recv[j].astype(F32)
+    err_all[me] = (scale * (recon - acts_all[me].astype(F32))).astype(BF16)
+    share(err_all, err_ss, err_rs)
     cross(err_all.at[me], err_half, ehalf_ss, ehalf_rs)
 
     code_rows = [codes.astype(F32)]
@@ -252,11 +246,8 @@
     unit_gain = SPARSITY * scale * totals / norm_col
     codes_t = codes_t.astype(BF16)
 
-    grad = jnp.zeros((rows_group, lat), F32)
-    for cut, err in gather_cuts(err_all, err_ss, err_rs, lambda: spread(err_half, ehalf_ss, ehalf_rs)):
-        grad = grad + lax.dot_general(
-            err, dec_v[:, cut], (((1,), (1,)), ((), ())), preferred_element_type=F32
-        )
+    err = gather(err_all, err_ss, err_rs, lambda: spread(err_half, ehalf_ss, ehalf_rs))
+    grad = jnp.dot(err, dec_t[...], preferred_element_type=F32)
     grad = grad + SPARSITY * scale * norm_row
     grad_send[...] = grad.astype(BF16)
     for k, (p, d) in enumerate(z_peers):
@@ -270,7 +261,8 @@
 
     err_rows = [err_all[:, :, mine_cols].astype(F32).reshape(rows_group, half)]
     for q, p in enumerate(dp_peers):
-        for j in lat_peers:
+        with jax.named_scope("halves"):
+          for j in lat_peers:
             wait_half(err_half, ehalf_ss, ehalf_rs, p, j)
         err_rows.append(err_half[p].astype(F32).reshape(rows_group, half))
     err_rows = jnp.concatenate(err_rows, axis=0)
@@ -285,7 +277,8 @@
         gates.append(gate_recv[d].astype(F32))
 
     def wait_grad(p, d):
-        remote(grad_send, grad_recv.at[p, d], grad_ss.at[0], grad_rs.at[p, d], "latent", partner).wait_recv()
+        with jax.named_scope("zgrad"):
+          remote(grad_send, grad_recv.at[p, d], grad_ss.at[0], grad_rs.at[p, d], "latent", partner).wait_recv()
         return grad_recv[p, d].astype(F32)
 
     for p in layer_peers:
@@ -303,7 +296,8 @@
     for d in range(1, n_dp):
         bias_mine = jnp.where(group == d, bias_sum[:, d * lat_part : (d + 1) * lat_part], bias_mine)
     eb_stage[...] = bias_mine.reshape(lat_part)
-    for copy in sent:
+    with jax.named_scope("sends"):
+      for copy in sent:
         copy.wait_send()
 
 
@@ -339,7 +333,6 @@
     tiles, blocks = block_ids.shape[1:]
     group_rows = rows * n_lat
     chips = n_lat // CORES
-    splits = SPLITS if width % (128 * SPLITS) == 0 else 1
     half = width // n_dp
     any_spec = pl.BlockSpec(memory_space=pltpu.HBM)
     vmem_spec = pl.BlockSpec(memory_space=pltpu.VMEM)
@@ -363,15 +356,16 @@
             pltpu.VMEM((1, width), F32),
             pltpu.VMEM((blocks, tiles), jnp.int32),
             pltpu.VMEM((1, tiles), jnp.int32),
+            pltpu.VMEM((width, lat), BF16),
             pltpu.VMEM((n_dp, n_lat, rows, half), BF16),
             pltpu.VMEM((group_rows, lat), BF16),
             pltpu.VMEM((n_layer, group_rows, lat), BF16),
             pltpu.VMEM((group_rows, lat), BF16),
             pltpu.VMEM((n_dp, group_rows, lat), BF16),
-            pltpu.VMEM((CORES, chips, rows, width), BF16),
+            pltpu.VMEM((n_lat, rows, width), BF16),
             pltpu.VMEM((chips, rows, width), BF16),
             pltpu.VMEM((chips, rows, width), BF16),
-            pltpu.VMEM((chips, rows, width), BF16),
+            pltpu.VMEM((n_lat, rows, width), BF16),
             pltpu.VMEM((n_lat, rows, width), BF16),
             pltpu.VMEM((n_dp, n_lat, rows, half), BF16),
             pltpu.VMEM((group_rows, lat), BF16),
@@ -379,13 +373,13 @@
             pltpu.VMEM((group_rows, lat), BF16),
             pltpu.VMEM((n_dp, group_rows, lat), BF16),
             dma(7),
-            dma(2 * chips - 1, splits), dma(n_lat, splits),
+            dma(2 * chips - 1), dma(n_lat),
             dma(n_dp - 1, n_lat), dma(n_dp, n_lat),
             dma(n_layer - 1), dma(n_layer),
             dma(n_dp - 1), dma(n_dp),
-            dma(splits), dma(splits),
-            dma(chips - 1, splits), dma(chips, splits),
-            dma(2 * chips - 1, splits), dma(n_lat, splits),
+            dma(chips), dma(chips),
+            dma(n_lat), dma(n_lat),
+            dma(2 * chips - 1), dma(n_lat),
             dma(n_dp - 1, n_lat), dma(n_dp, n_lat),
             dma(n_layer * n_dp - 1), dma(n_layer, n_dp),
             dma(n_dp - 1), dma(n_dp),

time: 32 us -> 31 us (0.969)
  Pallas kernels: 31.2 us -> 30.2 us
    pallas_call x1, Pallas kernels: 30.1 us -> 29.1 us  [on_device(): pl.pallas_call(functools.partial(step_kernel, n_layer, n_lat, n_dp), out_...]
where the time goes in v2:
time: 31 us; the launch traced here: 30.8 us
  Pallas kernels  30.2 us (97%)
  between operations  0.64 us (2%)
    pallas_call x1, Pallas kernels, on_device(): pl.pallas_call(functools.partial(step_kernel, n_layer, n_lat, n_dp), out_...  29.1 us
    pallas_call x1, Pallas kernels, on_device(): pl.pallas_call(finish_kernel, out_shape=(jax.ShapeDtypeStruct((1, half, l...  1.12 us

profile of v2, /device:TPU:0, one launch (start us, length us, event | category | flops | bytes accessed | tf_op | source)
XLA Modules:
  0.0 30.8 jit_solution(4925205646597097206)
XLA Ops:
  0.6 29.1 %crosscoder_step.1 = (bf16[1280,128]{1,0:T(8,128)(2,1)S(1)}, bf16[128,256]{1,0:T(8,128)(2,1)S(1)}, bf16[256,1280]{1,0:T(8,128)(2,1)S(1)}, f32[128]{0:T(128)S(1)}, f32[1,1280]{1,0:T(1,128)S(1)}) custom-call(bf16[1,8,2560]{2,1,0:T(8,128)(2,1)} %acts_hbm.1, bf16[1,2560,256]{2,1,0:T(8,128)(2,1)} %enc_hbm.1, bf16[1,256,2560]{2,1,0:T(8,128)(2,1)} %dec_hbm.1, ...), custom_call_target="tpu_custom_call" | custom-call | tf_op jit(solution)/shard_map/crosscoder_step/pallas_call | solution.py:340
  29.7 1.1 %crosscoder_finish.1 = (bf16[1,1280,256]{2,1,0:T(8,128)(2,1)}, bf16[1,256,1280]{2,1,0:T(8,128)(2,1)}, f32[128]{0:T(128)}, f32[1,1280]{1,0:T(1,128)}) custom-call(bf16[1280,128]{1,0:T(8,128)(2,1)S(1)} %get-tuple-element.9.acts_t, bf16[128,256]{1,0:T(8,128)(2,1)S(1)} %get-tuple-element.10.pg_rows, bf16[256,1280]{1,0:T(8,128)(2,1)S(1)} %get-tuple-element.11.dec_grad, ...), custom_call_target="tpu_custom_call" | custom-call | tf_op jit(solution)/shard_map/crosscoder_finish/pallas_call | solution.py:398

commit v3 on v2

--- a/solution.py
+++ b/solution.py
@@ -38,8 +38,8 @@
     dec_t, acts_half, pre_send, pre_recv, codes_send, codes_recv,
     part_send, pair_recv, chip_send, part_recv, err_all, err_half, grad_send, grad_recv,
     gate_send, gate_recv,
-    in_sems, acts_ss, acts_rs, ahalf_ss, ahalf_rs, pre_ss, pre_rs, codes_ss, codes_rs,
-    pair_ss, pair_rs, part_ss, part_rs, err_ss, err_rs, ehalf_ss, ehalf_rs, grad_ss, grad_rs, gate_ss, gate_rs,
+    in_sems, send_sem, acts_rs, ahalf_rs, pre_rs, codes_rs,
+    pair_rs, part_rs, err_rs, ehalf_rs, grad_rs, gate_rs,
 ):
     layer = lax.axis_index("layer")
     me = lax.axis_index("latent")
@@ -88,14 +88,16 @@
     barrier = pltpu.get_barrier_semaphore()
     for p in lat_peers:
         pl.semaphore_signal(barrier, inc=1, device_id={"latent": p}, device_id_type=MESH)
-    for p, d in z_peers:
-        pl.semaphore_signal(barrier, inc=1, device_id={"layer": p, "dp": d}, device_id_type=MESH)
+    for p in layer_peers:
+        pl.semaphore_signal(barrier, inc=1, device_id={"layer": p}, device_id_type=MESH)
+    for p in dp_peers:
+        pl.semaphore_signal(barrier, inc=1, device_id={"dp": p}, device_id_type=MESH)
     with jax.named_scope("entry"):
-        pl.semaphore_wait(barrier, len(lat_peers) + len(z_peers))
-
-    def remote(src, dst, ss, rs, axis, peer):
+        pl.semaphore_wait(barrier, n_lat + n_layer + n_dp - 3)
+
+    def remote(src, dst, rs, axis, peer):
         return pltpu.make_async_remote_copy(
-            src_ref=src, dst_ref=dst, send_sem=ss, recv_sem=rs,
+            src_ref=src, dst_ref=dst, send_sem=send_sem.at[0], recv_sem=rs,
             device_id={axis: peer}, device_id_type=MESH,
         )
 
@@ -106,38 +108,38 @@
         copy.start()
         sent.append(copy)
 
-    def share(buf, ss, rs):
+    def share(buf, rs):
         mine = buf.at[me]
         targets = [q * CORES + 1 - core for q in chip_peers] + [partner]
         for k, j in enumerate(targets):
-            send(mine, mine, ss.at[k], rs.at[me], "latent", j)
-
-    def wait_block(buf, ss, rs, j):
-        remote(buf.at[j], buf.at[j], ss.at[0], rs.at[j], "latent", partner).wait_recv()
-
-    def gather(buf, ss, rs, beside):
+            send(mine, mine, rs.at[me], "latent", j)
+
+    def wait_block(buf, rs, j):
+        remote(buf.at[j], buf.at[j], rs.at[j], "latent", partner).wait_recv()
+
+    def gather(buf, rs, beside):
         for k, q in enumerate(chip_peers):
             j = q * CORES + 1 - core
             with jax.named_scope("relay"):
-                wait_block(buf, ss, rs, j)
-            send(buf.at[j], buf.at[j], ss.at[n_peers + 1 + k], rs.at[j], "latent", partner)
+                wait_block(buf, rs, j)
+            send(buf.at[j], buf.at[j], rs.at[j], "latent", partner)
         beside()
         with jax.named_scope("direct"):
             for j in [partner]:
-                wait_block(buf, ss, rs, j)
+                wait_block(buf, rs, j)
         with jax.named_scope("relayed"):
             for q in chip_peers:
-                wait_block(buf, ss, rs, q * CORES + core)
+                wait_block(buf, rs, q * CORES + core)
         return buf[...].astype(F32).reshape(rows_group, width).astype(BF16)
 
-    def cross(src, dst_half, ss, rs):
+    def cross(src, dst_half, rs):
         for q, p in enumerate(dp_peers):
             cols = pl.ds(pl.multiple_of(p * half, 128), half)
-            send(src.at[:, cols], dst_half.at[group, me], ss.at[q, 0], rs.at[group, me], "dp", p)
+            send(src.at[:, cols], dst_half.at[group, me], rs.at[group, me], "dp", p)
 
     own_acts.wait()
-    share(acts_all, acts_ss, acts_rs)
-    cross(acts_all.at[me], acts_half, ahalf_ss, ahalf_rs)
+    share(acts_all, acts_rs)
+    cross(acts_all.at[me], acts_half, ahalf_rs)
 
     for load in loads:
         load.wait()
@@ -165,28 +167,28 @@
         )
         mask = jnp.where(lat_block == b, jnp.broadcast_to(row_hit, (rows_group, lat)), mask)
 
-    def wait_half(dst_half, ss, rs, p, j):
+    def wait_half(dst_half, rs, p, j):
         remote(
-            dst_half.at[p, j], dst_half.at[p, j], ss.at[0, 0], rs.at[p, j], "latent", lat_peers[0]
+            dst_half.at[p, j], dst_half.at[p, j], rs.at[p, j], "latent", lat_peers[0]
         ).wait_recv()
 
-    def spread(dst_half, ss, rs):
+    def spread(dst_half, rs):
         for q, p in enumerate(dp_peers):
             with jax.named_scope("half"):
-                wait_half(dst_half, ss, rs, p, me)
+                wait_half(dst_half, rs, p, me)
             for k, j in enumerate(lat_peers):
-                send(dst_half.at[p, me], dst_half.at[p, me], ss.at[q, k + 1], rs.at[p, me], "latent", j)
-
-    gathered = gather(acts_all, acts_ss, acts_rs, lambda: None)
+                send(dst_half.at[p, me], dst_half.at[p, me], rs.at[p, me], "latent", j)
+
+    gathered = gather(acts_all, acts_rs, lambda: None)
     pre = jnp.dot(gathered, enc_v[...], preferred_element_type=F32)
     pre_send[...] = pre.astype(BF16)
     for k, p in enumerate(layer_peers):
-        send(pre_send, pre_recv.at[layer], pre_ss.at[k], pre_rs.at[layer], "layer", p)
-    spread(acts_half, ahalf_ss, ahalf_rs)
+        send(pre_send, pre_recv.at[layer], pre_rs.at[layer], "layer", p)
+    spread(acts_half, ahalf_rs)
     pre = pre + ebias_v[...][None, :]
     for k, p in enumerate(layer_peers):
         with jax.named_scope("layers"):
-            remote(pre_send, pre_recv.at[p], pre_ss.at[k], pre_rs.at[p], "layer", p).wait_recv()
+            remote(pre_send, pre_recv.at[p], pre_rs.at[p], "layer", p).wait_recv()
         pre = pre + pre_recv[p].astype(F32)
 
     codes = (jax.nn.softplus(pre) * mask).astype(BF16)
@@ -196,64 +198,68 @@
     for k, q in enumerate(chip_peers):
         send(
             part_send.at[q * CORES + core], pair_recv.at[k],
-            pair_ss.at[k], pair_rs.at[k], "latent", partner,
+            pair_rs.at[k], "latent", partner,
         )
     for k, j in enumerate([partner]):
-        send(part_send.at[j], part_recv.at[me], part_ss.at[n_peers + k], part_rs.at[me], "latent", j)
+        send(part_send.at[j], part_recv.at[me], part_rs.at[me], "latent", j)
     for k, q in enumerate(chip_peers):
         with jax.named_scope("pair"):
             remote(
-                pair_recv.at[k], pair_recv.at[k], pair_ss.at[k], pair_rs.at[k], "latent", partner
+                pair_recv.at[k], pair_recv.at[k], pair_rs.at[k], "latent", partner
             ).wait_recv()
         total = part_send[q * CORES + 1 - core].astype(F32) + pair_recv[k].astype(F32)
         chip_send[k] = total.astype(BF16)
         send(
-            chip_send.at[k], part_recv.at[me], part_ss.at[k], part_rs.at[me],
+            chip_send.at[k], part_recv.at[me], part_rs.at[me],
             "latent", q * CORES + 1 - core,
         )
     for k, p in enumerate(dp_peers):
-        send(codes_send, codes_recv.at[group], codes_ss.at[k], codes_rs.at[group], "dp", p)
+        send(codes_send, codes_recv.at[group], codes_rs.at[group], "dp", p)
 
     mine_cols = pl.ds(pl.multiple_of(group * half, 128), half)
     acts_rows = [acts_all[:, :, mine_cols].astype(F32).reshape(rows_group, half)]
     for q, p in enumerate(dp_peers):
         with jax.named_scope("halves"):
           for j in lat_peers:
-            wait_half(acts_half, ahalf_ss, ahalf_rs, p, j)
+            wait_half(acts_half, ahalf_rs, p, j)
         acts_rows.append(acts_half[p].astype(F32).reshape(rows_group, half))
     acts_t[...] = jnp.concatenate(acts_rows, axis=0).T.astype(BF16)
 
     gate = mask * jax.nn.sigmoid(pre)
     gate_send[...] = gate.astype(BF16)
     for k, p in enumerate(dp_peers):
-        send(gate_send, gate_recv.at[group], gate_ss.at[k], gate_rs.at[group], "dp", p)
+        send(gate_send, gate_recv.at[group], gate_rs.at[group], "dp", p)
 
     recon = part_send[me].astype(F32) + dbias_v[...]
     for j in [partner] + [q * CORES + 1 - core for q in chip_peers]:
         with jax.named_scope("chips"):
-            wait_block(part_recv, part_ss, part_rs, j)
+            wait_block(part_recv, part_rs, j)
         recon = recon + part_recv[j].astype(F32)
     err_all[me] = (scale * (recon - acts_all[me].astype(F32))).astype(BF16)
-    share(err_all, err_ss, err_rs)
-    cross(err_all.at[me], err_half, ehalf_ss, ehalf_rs)
+    share(err_all, err_rs)
+    cross(err_all.at[me], err_half, ehalf_rs)
 
     code_rows = [codes.astype(F32)]
     for k, p in enumerate(dp_peers):
-        remote(codes_send, codes_recv.at[p], codes_ss.at[k], codes_rs.at[p], "dp", p).wait_recv()
+        remote(codes_send, codes_recv.at[p], codes_rs.at[p], "dp", p).wait_recv()
         code_rows.append(codes_recv[p].astype(F32))
     codes_t = jnp.concatenate(code_rows, axis=0).T
     totals = jnp.sum(codes_t, axis=1, keepdims=True)
     unit_gain = SPARSITY * scale * totals / norm_col
     codes_t = codes_t.astype(BF16)
 
-    err = gather(err_all, err_ss, err_rs, lambda: spread(err_half, ehalf_ss, ehalf_rs))
+    err = gather(err_all, err_rs, lambda: spread(err_half, ehalf_rs))
     grad = jnp.dot(err, dec_t[...], preferred_element_type=F32)
     grad = grad + SPARSITY * scale * norm_row
     grad_send[...] = grad.astype(BF16)
+    gates = [gate]
+    for k, d in enumerate(dp_peers):
+        remote(gate_send, gate_recv.at[d], gate_rs.at[d], "dp", d).wait_recv()
+        gates.append(gate_recv[d].astype(F32))
     for k, (p, d) in enumerate(z_peers):
         copy = pltpu.make_async_remote_copy(
             src_ref=grad_send, dst_ref=grad_recv.at[layer, group],
-            send_sem=grad_ss.at[k], recv_sem=grad_rs.at[layer, group],
+            send_sem=send_sem.at[0], recv_sem=grad_rs.at[layer, group],
             device_id={"layer": p, "dp": d}, device_id_type=MESH,
         )
         copy.start()
@@ -263,7 +269,7 @@
     for q, p in enumerate(dp_peers):
         with jax.named_scope("halves"):
           for j in lat_peers:
-            wait_half(err_half, ehalf_ss, ehalf_rs, p, j)
+            wait_half(err_half, ehalf_rs, p, j)
         err_rows.append(err_half[p].astype(F32).reshape(rows_group, half))
     err_rows = jnp.concatenate(err_rows, axis=0)
     db_stage[...] = jnp.sum(err_rows, axis=0, keepdims=True)
@@ -271,14 +277,9 @@
     dec_grad = dec_grad + unit_gain * dec_v[:, mine_cols].astype(F32)
     dec_stage[...] = dec_grad.astype(BF16)
 
-    gates = [gate]
-    for k, d in enumerate(dp_peers):
-        remote(gate_send, gate_recv.at[d], gate_ss.at[k], gate_rs.at[d], "dp", d).wait_recv()
-        gates.append(gate_recv[d].astype(F32))
-
     def wait_grad(p, d):
         with jax.named_scope("zgrad"):
-          remote(grad_send, grad_recv.at[p, d], grad_ss.at[0], grad_rs.at[p, d], "latent", partner).wait_recv()
+          remote(grad_send, grad_recv.at[p, d], grad_rs.at[p, d], "latent", partner).wait_recv()
         return grad_recv[p, d].astype(F32)
 
     for p in layer_peers:
@@ -372,17 +373,10 @@
             pltpu.VMEM((n_layer, n_dp, group_rows, lat), BF16),
             pltpu.VMEM((group_rows, lat), BF16),
             pltpu.VMEM((n_dp, group_rows, lat), BF16),
-            dma(7),
-            dma(2 * chips - 1), dma(n_lat),
-            dma(n_dp - 1, n_lat), dma(n_dp, n_lat),
-            dma(n_layer - 1), dma(n_layer),
-            dma(n_dp - 1), dma(n_dp),
-            dma(chips), dma(chips),
-            dma(n_lat), dma(n_lat),
-            dma(2 * chips - 1), dma(n_lat),
-            dma(n_dp - 1, n_lat), dma(n_dp, n_lat),
-            dma(n_layer * n_dp - 1), dma(n_layer, n_dp),
-            dma(n_dp - 1), dma(n_dp),
+            dma(7), dma(1),
+            dma(n_lat), dma(n_dp, n_lat), dma(n_layer), dma(n_dp),
+            dma(chips), dma(n_lat), dma(n_lat), dma(n_dp, n_lat),
+            dma(n_layer, n_dp), dma(n_dp),
         ],
         compiler_params=pltpu.CompilerParams(
             collective_id=0, has_side_effects=True, vmem_limit_bytes=40 << 20

time: 31 us -> 30.2 us (0.974)
  Pallas kernels: 30.2 us -> 29.4 us
    pallas_call x1, Pallas kernels: 29.1 us -> 28.3 us  [on_device(): pl.pallas_call(functools.partial(step_kernel, n_layer, n_lat, n_dp), out_...]
where the time goes in v3:
time: 30.2 us; the launch traced here: 30.1 us
  Pallas kernels  29.4 us (97%)
  between operations  0.64 us (2%)
    pallas_call x1, Pallas kernels, on_device(): pl.pallas_call(functools.partial(step_kernel, n_layer, n_lat, n_dp), out_...  28.3 us
    pallas_call x1, Pallas kernels, on_device(): pl.pallas_call(finish_kernel, out_shape=(jax.ShapeDtypeStruct((1, half, l...  1.12 us

profile of v3, /device:TPU:0, one launch (start us, length us, event | category | flops | bytes accessed | tf_op | source)
XLA Modules:
  0.0 30.1 jit_solution(5700864435109474692)
XLA Ops:
  0.6 28.3 %crosscoder_step.1 = (bf16[1280,128]{1,0:T(8,128)(2,1)S(1)}, bf16[128,256]{1,0:T(8,128)(2,1)S(1)}, bf16[256,1280]{1,0:T(8,128)(2,1)S(1)}, f32[128]{0:T(128)S(1)}, f32[1,1280]{1,0:T(1,128)S(1)}) custom-call(bf16[1,8,2560]{2,1,0:T(8,128)(2,1)} %acts_hbm.1, bf16[1,2560,256]{2,1,0:T(8,128)(2,1)} %enc_hbm.1, bf16[1,256,2560]{2,1,0:T(8,128)(2,1)} %dec_hbm.1, ...), custom_call_target="tpu_custom_call" | custom-call | tf_op jit(solution)/shard_map/crosscoder_step/pallas_call | solution.py:341
  29.0 1.1 %crosscoder_finish.1 = (bf16[1,1280,256]{2,1,0:T(8,128)(2,1)}, bf16[1,256,1280]{2,1,0:T(8,128)(2,1)}, f32[128]{0:T(128)}, f32[1,1280]{1,0:T(1,128)}) custom-call(bf16[1280,128]{1,0:T(8,128)(2,1)S(1)} %get-tuple-element.9.acts_t, bf16[128,256]{1,0:T(8,128)(2,1)S(1)} %get-tuple-element.10.pg_rows, bf16[256,1280]{1,0:T(8,128)(2,1)S(1)} %get-tuple-element.11.dec_grad, ...), custom_call_target="tpu_custom_call" | custom-call | tf_op jit(solution)/shard_map/crosscoder_finish/pallas_call | solution.py:392

commit v4 on v3

--- a/solution.py
+++ b/solution.py
@@ -70,8 +70,8 @@
     own_acts = pltpu.make_async_copy(acts_hbm.at[0], acts_all.at[me], in_sems.at[0])
     own_acts.start()
     loads = [
-        pltpu.make_async_copy(src, dst, in_sems.at[i + 1])
-        for i, (src, dst) in enumerate(
+        pltpu.make_async_copy(src, dst, in_sems.at[1])
+        for _, (src, dst) in enumerate(
             (
                 (enc_hbm.at[0], enc_v),
                 (dec_hbm.at[0], dec_v),
@@ -135,7 +135,7 @@
     def cross(src, dst_half, rs):
         for q, p in enumerate(dp_peers):
             cols = pl.ds(pl.multiple_of(p * half, 128), half)
-            send(src.at[:, cols], dst_half.at[group, me], rs.at[group, me], "dp", p)
+            send(src.at[:, cols], dst_half.at[group, me], rs.at[group, 0], "dp", p)
 
     own_acts.wait()
     share(acts_all, acts_rs)
@@ -167,17 +167,18 @@
         )
         mask = jnp.where(lat_block == b, jnp.broadcast_to(row_hit, (rows_group, lat)), mask)
 
-    def wait_half(dst_half, rs, p, j):
-        remote(
-            dst_half.at[p, j], dst_half.at[p, j], rs.at[p, j], "latent", lat_peers[0]
-        ).wait_recv()
+    def wait_halves(dst_half, rs, p):
+        blocks_in = dst_half.at[p, pl.ds(0, n_lat - 1)]
+        remote(blocks_in, blocks_in, rs.at[p, 1], "latent", lat_peers[0]).wait_recv()
 
     def spread(dst_half, rs):
         for q, p in enumerate(dp_peers):
             with jax.named_scope("half"):
-                wait_half(dst_half, rs, p, me)
+                remote(
+                    dst_half.at[p, me], dst_half.at[p, me], rs.at[p, 0], "dp", p
+                ).wait_recv()
             for k, j in enumerate(lat_peers):
-                send(dst_half.at[p, me], dst_half.at[p, me], rs.at[p, me], "latent", j)
+                send(dst_half.at[p, me], dst_half.at[p, me], rs.at[p, 1], "latent", j)
 
     gathered = gather(acts_all, acts_rs, lambda: None)
     pre = jnp.dot(gathered, enc_v[...], preferred_element_type=F32)
@@ -220,8 +221,7 @@
     acts_rows = [acts_all[:, :, mine_cols].astype(F32).reshape(rows_group, half)]
     for q, p in enumerate(dp_peers):
         with jax.named_scope("halves"):
-          for j in lat_peers:
-            wait_half(acts_half, ahalf_rs, p, j)
+            wait_halves(acts_half, ahalf_rs, p)
         acts_rows.append(acts_half[p].astype(F32).reshape(rows_group, half))
     acts_t[...] = jnp.concatenate(acts_rows, axis=0).T.astype(BF16)
 
@@ -268,8 +268,7 @@
     err_rows = [err_all[:, :, mine_cols].astype(F32).reshape(rows_group, half)]
     for q, p in enumerate(dp_peers):
         with jax.named_scope("halves"):
-          for j in lat_peers:
-            wait_half(err_half, ehalf_rs, p, j)
+            wait_halves(err_half, ehalf_rs, p)
         err_rows.append(err_half[p].astype(F32).reshape(rows_group, half))
     err_rows = jnp.concatenate(err_rows, axis=0)
     db_stage[...] = jnp.sum(err_rows, axis=0, keepdims=True)
@@ -373,9 +372,9 @@
             pltpu.VMEM((n_layer, n_dp, group_rows, lat), BF16),
             pltpu.VMEM((group_rows, lat), BF16),
             pltpu.VMEM((n_dp, group_rows, lat), BF16),
-            dma(7), dma(1),
-            dma(n_lat), dma(n_dp, n_lat), dma(n_layer), dma(n_dp),
-            dma(chips), dma(n_lat), dma(n_lat), dma(n_dp, n_lat),
+            dma(2), dma(1),
+            dma(n_lat), dma(n_dp, 2), dma(n_layer), dma(n_dp),
+            dma(chips), dma(n_lat), dma(n_lat), dma(n_dp, 2),
             dma(n_layer, n_dp), dma(n_dp),
         ],
         compiler_params=pltpu.CompilerParams(

time: 30.2 us -> 30 us (level)
  no operation moved by 1% of the time
where the time goes in v4:
time: 30 us; the launch traced here: 29.8 us
  Pallas kernels  29.2 us (97%)
  between operations  0.64 us (2%)
    pallas_call x1, Pallas kernels, on_device(): pl.pallas_call(functools.partial(step_kernel, n_layer, n_lat, n_dp), out_...  28.1 us
    pallas_call x1, Pallas kernels, on_device(): pl.pallas_call(finish_kernel, out_shape=(jax.ShapeDtypeStruct((1, half, l...  1.12 us

profile of v4, /device:TPU:0, one launch (start us, length us, event | category | flops | bytes accessed | tf_op | source)
XLA Modules:
  0.0 29.8 jit_solution(7545130100632296910)
XLA Ops:
  0.6 28.1 %crosscoder_step.1 = (bf16[1280,128]{1,0:T(8,128)(2,1)S(1)}, bf16[128,256]{1,0:T(8,128)(2,1)S(1)}, bf16[256,1280]{1,0:T(8,128)(2,1)S(1)}, f32[128]{0:T(128)S(1)}, f32[1,1280]{1,0:T(1,128)S(1)}) custom-call(bf16[1,8,2560]{2,1,0:T(8,128)(2,1)} %acts_hbm.1, bf16[1,2560,256]{2,1,0:T(8,128)(2,1)} %enc_hbm.1, bf16[1,256,2560]{2,1,0:T(8,128)(2,1)} %dec_hbm.1, ...), custom_call_target="tpu_custom_call" | custom-call | tf_op jit(solution)/shard_map/crosscoder_step/pallas_call | solution.py:340
  28.7 1.1 %crosscoder_finish.1 = (bf16[1,1280,256]{2,1,0:T(8,128)(2,1)}, bf16[1,256,1280]{2,1,0:T(8,128)(2,1)}, f32[128]{0:T(128)}, f32[1,1280]{1,0:T(1,128)}) custom-call(bf16[1280,128]{1,0:T(8,128)(2,1)S(1)} %get-tuple-element.9.acts_t, bf16[128,256]{1,0:T(8,128)(2,1)S(1)} %get-tuple-element.10.pg_rows, bf16[256,1280]{1,0:T(8,128)(2,1)S(1)} %get-tuple-element.11.dec_grad, ...), custom_call_target="tpu_custom_call" | custom-call | tf_op jit(solution)/shard_map/crosscoder_finish/pallas_call | solution.py:391
